TPU v7x, 32 devices: a whole 2x2x4 slice. The times are simulated.
32 devices in a mesh: grp: 2 (over y), dp: 16 (over z, x, core).
Axes of the slice: x: 2, y: 2, z: 4, core: 2. Of those that a mesh axis runs over, the one named last changes fastest.
Arguments:
- teacher_states: bfloat16 [2, 4096, 6144], P(None, 'dp', 'grp'), may hold values from -18.5 to 18.5
- student_features: bfloat16 [2, 4096, 1024], P(None, 'dp'), may hold values from -13 to 13
- w_first: bfloat16 [1024, 1024], replicated, may hold values from -0.1875 to 0.1875
- w_second: bfloat16 [1024, 1024], replicated, may hold values from -0.1875 to 0.1875
Outputs:
- correlation: float32 [1024, 6144], P('dp', 'grp')
All inputs are finite; a program needn't handle non-finite values.
Results may differ from a plain program's by a relative error of at most 0.0003.
Values may be sent and summed in bfloat16 or wider, within the bound.
No kernel may reach another device: no remote copies, remote signals or barrier semaphores. Data moves between devices by JAX's collectives and lax.ppermute only.
A program may use at most 128 MiB of HBM per device.

v0:
```python
import math
import jax
import jax.numpy as jnp
from jax import lax
from jax.sharding import PartitionSpec as P

DT = 6144
EPSILON = 1e-06


def normalize_rows(states):
    values = states.astype(jnp.float32)
    sums = (jnp.sum(values, axis=1), jnp.sum(values * values, axis=1))
    totals = lax.psum((sums[0], sums[1]), "grp")
    row_mean = totals[0] / DT
    row_var = totals[1] / DT - row_mean * row_mean
    return (values - row_mean[:, None]) * lax.rsqrt(row_var + EPSILON)[:, None]


def teacher_side(states, token_total):
    normed = normalize_rows(states)
    power = lax.psum(jnp.sum(normed * normed, axis=0), "dp")
    return (normed * lax.rsqrt(power / token_total + EPSILON)).astype(jnp.bfloat16)


def project(features, w_first, w_second):
    hidden = jax.nn.gelu(jnp.dot(features, w_first, preferred_element_type=jnp.float32)).astype(
        jnp.bfloat16
    )
    return jnp.dot(hidden, w_second, preferred_element_type=jnp.float32)


def column_sums(projected):
    sums = (jnp.sum(projected, axis=0), jnp.sum(projected * projected, axis=0))
    return lax.psum((sums[0], sums[1]), "dp")


def standardize(projected, totals, token_total):
    col_mean = totals[0] / token_total
    col_var = totals[1] / token_total - col_mean * col_mean
    return ((projected - col_mean) * lax.rsqrt(col_var + EPSILON)).astype(jnp.bfloat16)


def student_side(features, w_first, w_second, token_total):
    projected = project(features, w_first, w_second)
    return standardize(projected, column_sums(projected), token_total)


def make_product(pair_list):
    running = None
    for student_z, teacher_z in pair_list:
        product = lax.dot_general(
            student_z, teacher_z, (((0,), (0,)), ((), ())), preferred_element_type=jnp.float32
        )
        running = product
    return running


def shards(teacher_states, student_features, w_first, w_second):
    micro_count = teacher_states.shape[0]
    token_total = teacher_states.shape[1] * lax.axis_size("dp")
    correlation = None
    for batch_index in range(micro_count):
        teacher_z = teacher_side(teacher_states[batch_index], token_total)
        student_z = student_side(student_features[batch_index], w_first, w_second, token_total)
        portion_sum = lax.psum_scatter(
            make_product([(student_z, teacher_z)]), "dp", scatter_dimension=0, tiled=True
        )
        correlation = portion_sum if correlation is None else correlation + portion_sum
    return correlation * (1.0 / math.sqrt(micro_count * token_total))


def solution(mesh):
    placed = (P(None, "dp", "grp"), P(None, "dp", None), P(), P())
    return jax.shard_map(
        shards, mesh=mesh, in_specs=placed, out_specs=P("dp", "grp"), check_vma=False
    )
```

profile of v0, /device:TPU:0, one launch (start us, length us, event | category | flops | bytes accessed | tf_op | source)
XLA Modules:
  0.0 245.8 jit_solution(2058709502384886520)
XLA Ops:
  6.5 0.0 copy-start
  6.5 0.0 reduce-scatter.2.cloned.1.call-start
  6.5 1.9 fusion.15
  8.5 2.4 convert_reduce_fusion
  10.9 0.0 copy-done
  10.9 3.3 %fusion.83 = (f32[1024]{0:T(1024)S(1)}, f32[1024]{0:T(1024)S(1)}, f32[256,1024]{1,0:T(8,128)S(1)}) fusion(bf16[1024,1024]{1,0:T(8,128)(2,1)S(1)} %copy-done, bf16[1024,1024]{1,0:T(8,128)(2,1)} %param.6, bf16[2,256,1024]{2,1,0:T(8,128)(2,1)} %param.5), kind=kOutput, calls=%fused_computation.91 | convolution fusion | flops 1076885504 | bytes 5775360 | tf_op jit(solution)/shard_map/dot_general | solution.py:30
  14.1 4.2 %fusion.84 = (f32[1024]{0:T(1024)S(1)}, f32[1024]{0:T(1024)S(1)}, f32[256,1024]{1,0:T(8,128)}) fusion(bf16[1024,1024]{1,0:T(8,128)(2,1)S(1)} %copy-done, bf16[1024,1024]{1,0:T(8,128)(2,1)} %param.6, bf16[2,256,1024]{2,1,0:T(8,128)(2,1)} %param.5), kind=kOutput, calls=%fused_computation.92 | convolution fusion | flops 1076885504 | bytes 5775360 | tf_op jit(solution)/shard_map/dot_general | solution.py:30
  18.4 5.9 %all-reduce.2 = (f32[256]{0:T(256)S(1)}, f32[256]{0:T(256)S(1)}) all-reduce(f32[256]{0:T(256)S(1)} %fusion.15, f32[256]{0:T(256)S(1)} %get-tuple-element.7), channel_id=1, replica_groups=mesh['grp'=2,'dp'=16] {'grp'}, use_global_device_ids=true, to_apply=%region_18.0 | all-reduce | flops 512 | bytes 4096 | tf_op jit(solution)/shard_map/psum | solution.py:14
  24.2 2.8 %fusion.13 = (f32[3072]{0:T(1024)S(1)}, f32[256]{0:T(256)S(1)}) fusion(f32[256]{0:T(256)S(1)} %get-tuple-element.30, f32[256]{0:T(256)S(1)} %get-tuple-element.29, bf16[2,256,3072]{2,1,0:T(8,128)(2,1)} %param.4), kind=kLoop, calls=%fused_computation.18 | loop fusion | flops 6288128 | bytes 3161088 | tf_op jit(solution)/shard_map/reduce_sum | solution.py:22
  27.1 4.9 %all-reduce.1 = (f32[256]{0:T(256)S(1)}, f32[256]{0:T(256)S(1)}) all-reduce(f32[256]{0:T(256)S(1)} %get-tuple-element.6, f32[256]{0:T(256)S(1)} %get-tuple-element.8), channel_id=1, replica_groups=mesh['grp'=2,'dp'=16] {'grp'}, use_global_device_ids=true, to_apply=%region_7.0 | all-reduce | flops 512 | bytes 4096 | tf_op jit(solution)/shard_map/psum | solution.py:14
  32.0 2.1 fusion.7
  34.1 59.7 %all-reduce = (f32[3072]{0:T(1024)S(1)}, f32[1024]{0:T(1024)S(1)}, f32[1024]{0:T(1024)S(1)}, f32[3072]{0:T(1024)S(1)}, f32[1024]{0:T(1024)S(1)}, /*index=5*/f32[1024]{0:T(1024)S(1)}) all-reduce(f32[3072]{0:T(1024)S(1)} %fusion.7, f32[1024]{0:T(1024)S(1)} %get-tuple-element.12, ...), channel_id=1, replica_groups=mesh['grp'=2,'dp'=16] {'dp'}, use_global_device_ids=true, to_apply=%region_9.0 | all-reduce | flops 10240 | bytes 81920 | tf_op jit(solution)/shard_map/psum | solution.py:22
  93.8 0.0 copy-start.1
  93.8 3.9 %fusion.17 = f32[1024,3072]{1,0:T(8,128)S(1)} fusion(f32[3072]{0:T(1024)S(1)} %get-tuple-element.34, f32[256]{0:T(256)S(1)} %get-tuple-element.28, f32[256]{0:T(256)S(1)} %get-tuple-element.27, bf16[2,256,3072]{2,1,0:T(8,128)(2,1)} %param.4, f32[256,1024]{1,0:T(8,128)} %get-tuple-element.31, f32[1024]{0:T(1024)S(1)} %get-tuple-element.35, ...), kind=kOutput, calls=%fused_computation.21 | convolution fusion | flops 1615331328 | bytes 15226880 | tf_op jit(solution)/shard_map/dot_general | solution.py:52
  97.7 0.0 copy-done.1
  97.8 6.7 %convolution_add_fusion = f32[1024,3072]{1,0:T(8,128)} fusion(f32[1024,3072]{1,0:T(8,128)S(1)} %fusion.17, f32[3072]{0:T(1024)S(1)} %get-tuple-element.33, f32[256]{0:T(256)S(1)} %get-tuple-element.30, f32[256]{0:T(256)S(1)} %get-tuple-element.29, bf16[2,256,3072]{2,1,0:T(8,128)(2,1)S(1)} %copy-done.1, f32[256,1024]{1,0:T(8,128)S(1)} %get-tuple-element.32, ...), kind=kOutput, calls=%fused_computation | convolution fusion | flops 1618477056 | bytes 27809792 | tf_op jit(solution)/shard_map/dot_general | solution.py:52
  104.5 0.0 reduce-scatter.2.cloned.1.call-update
  104.5 132.4 %reduce-scatter.2.cloned.1.call-done = f32[64,3072]{1,0:T(8,128)} async-done(((f32[1024,3072]{1,0:T(8,128)}), f32[64,3072]{1,0:T(8,128)}) %reduce-scatter.2.cloned.1.call-update) | async-done | bytes 786448 | tf_op jit(solution)/shard_map/reduce_scatter | solution.py:66
  236.9 2.1 broadcast_multiply_fusion
  (4 shorter events, 0.0 us)
Async XLA Ops:
  6.5 4.3 %copy-start = (bf16[1024,1024]{1,0:T(8,128)(2,1)S(1)}, bf16[1024,1024]{1,0:T(8,128)(2,1)}, u32[]{:S(2)}) copy-start(bf16[1024,1024]{1,0:T(8,128)(2,1)} %param.7) | copy-start | bytes 6291460
  6.5 230.4 %reduce-scatter.2.cloned.1.call-start = ((), (), s32[]{:S(2)}) async-start(), calls=%async_computation.1 | async-start | bytes 13369344 | tf_op jit(solution)/shard_map/reduce_scatter | solution.py:66
  93.8 3.9 %copy-start.1 = (bf16[2,256,3072]{2,1,0:T(8,128)(2,1)S(1)}, bf16[2,256,3072]{2,1,0:T(8,128)(2,1)}, u32[]{:S(2)}) copy-start(bf16[2,256,3072]{2,1,0:T(8,128)(2,1)} %param.4) | copy-start | bytes 9437188
Sparse Core Ops, SparseCore 0:
  104.6 132.2 reduce-scatter.1
where the time goes:
time: 246 us
  waiting for transfers between devices  132 us (54%)
  blocking collectives  70.5 us (29%)
  matrix products  18.1 us (7%)
  between operations  13.4 us (5%)
  other arithmetic  11.4 us (5%)
    reduce_scatter x1, waiting for transfers between devices, shards(): lax.psum_scatter(make_product([(student_z, teacher_z)]), 'dp', scatter_di...  132 us
    psum x1, blocking collectives, teacher_side(): power = lax.psum(jnp.sum(normed * normed, axis=0), 'dp')  59.7 us
    psum x2, blocking collectives, normalize_rows(): totals = lax.psum((sums[0], sums[1]), 'grp')  10.8 us
    dot_general x2, matrix products, make_product(): lax.dot_general(student_z, teacher_z, (((0,), (0,)), ((), ())), preferred...  10.6 us
    dot_general x2, matrix products, project(): return jnp.dot(hidden, w_second, preferred_element_type=jnp.float32)  7.49 us
    reduce_sum x2, other arithmetic, teacher_side(): power = lax.psum(jnp.sum(normed * normed, axis=0), 'dp')  4.93 us
  transfers between devices with their start and end apart: 1, of which 1 were waited for; matrix products, arithmetic and copies ran while one was open for 0% of the time, Pallas kernels for 0%

commit v1 on v0

--- a/solution.py
+++ b/solution.py
@@ -19,7 +19,7 @@
 
 def teacher_side(states, token_total):
     normed = normalize_rows(states)
-    power = lax.psum(jnp.sum(normed * normed, axis=0), "dp")
+    power = jnp.sum(lax.all_gather(jnp.sum(normed * normed, axis=0), "dp"), axis=0)
     return (normed * lax.rsqrt(power / token_total + EPSILON)).astype(jnp.bfloat16)
 
 

time: 246 us -> 288 us (1.17)
  blocking collectives: 70.5 us -> 111 us
    all_gather x0 -> x2, blocking collectives: none -> 40.6 us  [teacher_side(): lax.all_gather(jnp.sum(normed * normed, axis=0), 'dp')]
where the time goes in v1:
time: 288 us
  waiting for transfers between devices  132 us (46%)
  blocking collectives  111 us (39%)
  matrix products  19.4 us (7%)
  between operations  13.5 us (5%)
  other arithmetic  11.4 us (4%)
    reduce_scatter x1, waiting for transfers between devices, shards(): lax.psum_scatter(make_product([(student_z, teacher_z)]), 'dp', scatter_di...  132 us
    psum x1, blocking collectives, column_sums(): return lax.psum((sums[0], sums[1]), 'dp')  59.1 us
    all_gather x2, blocking collectives, teacher_side(): lax.all_gather(jnp.sum(normed * normed, axis=0), 'dp')  40.6 us
    psum x2, blocking collectives, normalize_rows(): totals = lax.psum((sums[0], sums[1]), 'grp')  10.8 us
    dot_general x2, matrix products, make_product(): lax.dot_general(student_z, teacher_z, (((0,), (0,)), ((), ())), preferred...  10.7 us
    dot_general x2, matrix products, project(): return jnp.dot(hidden, w_second, preferred_element_type=jnp.float32)  8.67 us
  transfers between devices with their start and end apart: 1, of which 1 were waited for; matrix products, arithmetic and copies ran while one was open for 0% of the time, Pallas kernels for 0%

profile of v1, /device:TPU:0, one launch (start us, length us, event | category | flops | bytes accessed | tf_op | source)
XLA Modules:
  0.0 287.9 jit_solution(8588649382847250513)
XLA Ops:
  6.5 0.0 copy-start
  6.5 0.0 reduce-scatter.2.cloned.1.call-start
  6.5 1.9 fusion.15
  8.5 2.4 convert_reduce_fusion
  10.9 0.0 copy-done
  10.9 3.8 %fusion.83 = (f32[1024]{0:T(1024)}, f32[1024]{0:T(1024)}, f32[256,1024]{1,0:T(8,128)S(1)}) fusion(bf16[1024,1024]{1,0:T(8,128)(2,1)S(1)} %copy-done, bf16[1024,1024]{1,0:T(8,128)(2,1)} %param.6, bf16[2,256,1024]{2,1,0:T(8,128)(2,1)} %param.5), kind=kOutput, calls=%fused_computation.91 | convolution fusion | flops 1076885504 | bytes 5775360 | tf_op jit(solution)/shard_map/dot_general | solution.py:30
  14.7 4.8 %fusion.84 = (f32[1024]{0:T(1024)}, f32[1024]{0:T(1024)}, f32[256,1024]{1,0:T(8,128)}) fusion(bf16[1024,1024]{1,0:T(8,128)(2,1)S(1)} %copy-done, bf16[1024,1024]{1,0:T(8,128)(2,1)} %param.6, bf16[2,256,1024]{2,1,0:T(8,128)(2,1)} %param.5), kind=kOutput, calls=%fused_computation.92 | convolution fusion | flops 1076885504 | bytes 5775360 | tf_op jit(solution)/shard_map/dot_general | solution.py:30
  19.5 5.9 %all-reduce.2 = (f32[256]{0:T(256)S(1)}, f32[256]{0:T(256)S(1)}) all-reduce(f32[256]{0:T(256)S(1)} %fusion.15, f32[256]{0:T(256)S(1)} %get-tuple-element.7), channel_id=1, replica_groups=mesh['grp'=2,'dp'=16] {'grp'}, use_global_device_ids=true, to_apply=%region_18.0 | all-reduce | flops 512 | bytes 4096 | tf_op jit(solution)/shard_map/psum | solution.py:14
  25.4 2.8 fusion.13
  28.2 4.9 %all-reduce.1 = (f32[256]{0:T(256)S(1)}, f32[256]{0:T(256)S(1)}) all-reduce(f32[256]{0:T(256)S(1)} %get-tuple-element.6, f32[256]{0:T(256)S(1)} %get-tuple-element.8), channel_id=1, replica_groups=mesh['grp'=2,'dp'=16] {'grp'}, use_global_device_ids=true, to_apply=%region_7.0 | all-reduce | flops 512 | bytes 4096 | tf_op jit(solution)/shard_map/psum | solution.py:14
  33.2 0.0 copy-start.5
  33.2 0.0 copy-done.2
  33.2 0.6 copy-done.4
  33.8 0.0 copy-done.5
  33.8 2.1 fusion.7
  35.9 22.7 %all-gather = f32[49152]{0:T(1024)S(1)} all-gather(f32[3072]{0:T(1024)S(1)} %fusion.7), channel_id=2, replica_groups=mesh['grp'=2,'dp'=16] {'dp'}, dimensions={0}, use_global_device_ids=true | all-gather | bytes 208896 | tf_op jit(solution)/shard_map/all_gather | solution.py:22
  58.6 18.0 %all-gather.1 = f32[49152]{0:T(1024)S(1)} all-gather(f32[3072]{0:T(1024)S(1)} %get-tuple-element.5), channel_id=3, replica_groups=mesh['grp'=2,'dp'=16] {'dp'}, dimensions={0}, use_global_device_ids=true | all-gather | bytes 208896 | tf_op jit(solution)/shard_map/all_gather | solution.py:22
  76.7 59.1 %all-reduce = (f32[1024]{0:T(1024)S(1)}, f32[1024]{0:T(1024)S(1)}, f32[1024]{0:T(1024)S(1)}, f32[1024]{0:T(1024)S(1)}) all-reduce(f32[1024]{0:T(1024)} %get-tuple-element.12, f32[1024]{0:T(1024)} %get-tuple-element.11, f32[1024]{0:T(1024)} %get-tuple-element.10, f32[1024]{0:T(1024)} %get-tuple-element.9), channel_id=1, replica_groups=mesh['grp'=2,'dp'=16] {'dp'}, use_global_device_ids=true, to_apply=%region_3.0 | all-reduce | flops 4096 | bytes 32768 | tf_op jit(solution)/shard_map/psum | solution.py:35
  135.8 0.0 copy-start.1
  135.9 3.9 %fusion.17 = f32[1024,3072]{1,0:T(8,128)S(1)} fusion(f32[3072]{0:T(1024)S(1)} %add_rsqrt_fusion.1, f32[256]{0:T(256)} %copy-done.5, f32[256]{0:T(256)} %copy-done.4, bf16[2,256,3072]{2,1,0:T(8,128)(2,1)} %param.4, f32[256,1024]{1,0:T(8,128)} %get-tuple-element.29, f32[1024]{0:T(1024)S(1)} %get-tuple-element.24, f32[1024]{0:T(1024)S(1)} %get-tuple-element.23), kind=kOutput, calls=%fused_computation.21 | convolution fusion | flops 1615331328 | bytes 15226880 | tf_op jit(solution)/shard_map/dot_general | solution.py:52
  139.8 6.8 %convolution_add_fusion = f32[1024,3072]{1,0:T(8,128)} fusion(f32[1024,3072]{1,0:T(8,128)S(1)} %fusion.17, f32[3072]{0:T(1024)S(1)} %add_rsqrt_fusion, f32[256]{0:T(256)S(1)} %copy-done.3, f32[256]{0:T(256)S(1)} %get-tuple-element.27, bf16[2,256,3072]{2,1,0:T(8,128)(2,1)S(1)} %copy-done.1, f32[256,1024]{1,0:T(8,128)S(1)} %get-tuple-element.30, ...), kind=kOutput, calls=%fused_computation | convolution fusion | flops 1618477056 | bytes 27809792 | tf_op jit(solution)/shard_map/dot_general | solution.py:52
  146.6 0.0 reduce-scatter.2.cloned.1.call-update
  146.6 132.4 %reduce-scatter.2.cloned.1.call-done = f32[64,3072]{1,0:T(8,128)} async-done(((f32[1024,3072]{1,0:T(8,128)}), f32[64,3072]{1,0:T(8,128)}) %reduce-scatter.2.cloned.1.call-update) | async-done | bytes 786448 | tf_op jit(solution)/shard_map/reduce_scatter | solution.py:66
  279.0 2.1 broadcast_multiply_fusion
  (15 shorter events, 0.2 us)
Async XLA Ops:
  6.5 4.3 %copy-start = (bf16[1024,1024]{1,0:T(8,128)(2,1)S(1)}, bf16[1024,1024]{1,0:T(8,128)(2,1)}, u32[]{:S(2)}) copy-start(bf16[1024,1024]{1,0:T(8,128)(2,1)} %param.7) | copy-start | bytes 6291460
  6.5 272.4 %reduce-scatter.2.cloned.1.call-start = ((), (), s32[]{:S(2)}) async-start(), calls=%async_computation.1 | async-start | bytes 13369344 | tf_op jit(solution)/shard_map/reduce_scatter | solution.py:66
  25.4 7.8 %copy-start.2 = (f32[256]{0:T(256)}, f32[256]{0:T(256)S(1)}, u32[]{:S(2)}) copy-start(f32[256]{0:T(256)S(1)} %get-tuple-element.28) | copy-start | bytes 3076
  33.2 0.6 copy-start.4
  33.2 0.6 copy-start.5
  135.8 3.9 %copy-start.1 = (bf16[2,256,3072]{2,1,0:T(8,128)(2,1)S(1)}, bf16[2,256,3072]{2,1,0:T(8,128)(2,1)}, u32[]{:S(2)}) copy-start(bf16[2,256,3072]{2,1,0:T(8,128)(2,1)} %param.4) | copy-start | bytes 9437188
  135.8 3.9 %copy-start.3 = (f32[256]{0:T(256)S(1)}, f32[256]{0:T(256)}, u32[]{:S(2)}) copy-start(f32[256]{0:T(256)} %copy-done.2) | copy-start | bytes 3076
Sparse Core Ops, SparseCore 0:
  146.7 132.1 reduce-scatter.1
